TPU v7x, 256 devices: a whole 4x4x8 slice. The times are simulated.
256 devices in a mesh: seq: 32 (over x, z), head: 8 (over y, core).
Axes of the slice: x: 4, y: 4, z: 8, core: 2. Of those that a mesh axis runs over, the one named last changes fastest.
Arguments:
- query_projection: bfloat16 [8192, 4096], P(('seq', 'head')), may hold values from -6 to 6
- key_projection: bfloat16 [8192, 1024], P(('seq', 'head')), may hold values from -6 to 6
- value_projection: bfloat16 [8192, 1024], P(('seq', 'head')), may hold values from -6 to 6
- output_gradient: bfloat16 [8192, 4096], P(('seq', 'head')), may hold values from -6 to 6
- partners: int32 [64, 6], P('seq'), may hold values from -1 to 62, as said below
Outputs:
- attention: bfloat16 [8192, 4096], P('seq', 'head')
- grad_query: bfloat16 [8192, 4096], P('seq', 'head')
- key_gradient: bfloat16 [8192, 1024], P('seq', 'head')
- value_gradient: bfloat16 [8192, 1024], P('seq', 'head')
Inputs may be any that keep to these rules, and one draw needn't show every extreme that they name: For l < 1, partners[b, l] is -1 if b < 2**l, else a block at a distance of 2**l to 2**(l+1) - 1 blocks before b (not before block 0). For l = 1 + j, with g = b // 2 - 2**j, it is -1 if g < 0, else one of the blocks g * 2 to g * 2 + 1.
All inputs are finite; a program needn't handle non-finite values.
Results may differ from a plain program's by a relative error of at most 0.012.
Values may be sent and summed in bfloat16 or wider, within the bound.
No kernel may reach another device: no remote copies, remote signals or barrier semaphores. Data moves between devices by JAX's collectives and lax.ppermute only.
A program may use at most 64 MiB of HBM per device.

v0:
```python
import math
import jax
import jax.numpy as jnp
from jax import lax
from jax.sharding import PartitionSpec as P

HEAD_SIZE = 128
BLOCK_TOKENS = 128
masked_score = -1e30


def from_behind(value, axis, steps):
    count = lax.axis_size(axis)
    initial, last = (max(0, -steps), min(count, count - steps))
    return lax.ppermute(value, axis, [(source, source + steps) for source in range(initial, last)])


def shards(query_projection, key_projection, value_projection, output_gradient, partners):
    q_local, dout_local, k_local, v_local = (
        lax.all_to_all(query_projection, "head", split_axis=1, concat_axis=0, tiled=True),
        lax.all_to_all(output_gradient, "head", split_axis=1, concat_axis=0, tiled=True),
        lax.all_to_all(key_projection, "head", split_axis=1, concat_axis=0, tiled=True),
        lax.all_to_all(value_projection, "head", split_axis=1, concat_axis=0, tiled=True),
    )
    tokens_dev = q_local.shape[0]
    block_count = tokens_dev // BLOCK_TOKENS
    q_heads = q_local.shape[1] // HEAD_SIZE
    kv_heads = k_local.shape[1] // HEAD_SIZE
    heads_per_group = q_heads // kv_heads
    level_list = partners.shape[1]
    near_count = block_count.bit_length() - 1
    far_count = level_list - near_count
    scaling = 1.0 / math.sqrt(HEAD_SIZE)
    highest = lax.Precision.HIGHEST
    key_value = jnp.stack([k_local, v_local])
    far_sets = [from_behind(key_value, "seq", 2**degree) for degree in range(far_count)]
    block_shape = (2, block_count, BLOCK_TOKENS, kv_heads * HEAD_SIZE)
    own_blocks = key_value.reshape(block_shape)
    near_pool = jnp.concatenate([far_sets[0].reshape(block_shape), own_blocks], axis=1)
    first_block = lax.axis_index("seq") * block_count
    is_valid = partners >= 0
    picked = [own_blocks]
    degree = 0
    target = partners[:, degree] - first_block + block_count
    near_targets = target
    picked.append(jnp.take(near_pool, jnp.clip(target, 0, 2 * block_count - 1), axis=1))
    far_targets = []
    for degree in range(far_count):
        target = partners[:, near_count + degree] - (first_block - 2**degree * block_count)
        far_targets.append(target)
        picked.append(
            jnp.take(
                far_sets[degree].reshape(block_shape), jnp.clip(target, 0, block_count - 1), axis=1
            )
        )
    slot_count_all = 1 + level_list
    key_number = slot_count_all * BLOCK_TOKENS
    gathered = jnp.stack(picked, axis=2).reshape(2, block_count, key_number, kv_heads, HEAD_SIZE)
    row_ids = jnp.arange(BLOCK_TOKENS)[:, None]
    columns = jnp.arange(key_number)[None, :]
    slot_of = columns // BLOCK_TOKENS
    causal = (slot_of == 0) & (columns <= row_ids)
    slot_valid = jnp.concatenate([jnp.ones((block_count, 1), bool), is_valid], axis=1)
    allowed = causal[None] | (slot_of > 0)[None] & slot_valid[:, slot_of[0]][:, None, :]
    query_blocks = q_local.reshape(block_count, BLOCK_TOKENS, q_heads, HEAD_SIZE)
    output_grad_blocks = dout_local.reshape(block_count, BLOCK_TOKENS, q_heads, HEAD_SIZE)
    attn_list = []
    dquery_list = []
    key_row_set = gathered[0, :, :, 0, :]
    value_row_set = gathered[1, :, :, 0, :]
    key_sum = jnp.zeros((block_count, key_number, HEAD_SIZE), jnp.float32)
    value_sum = jnp.zeros((block_count, key_number, HEAD_SIZE), jnp.float32)
    for member in range(heads_per_group):
        query_row_set = query_blocks[:, :, member, :]
        output_grad_rows = output_grad_blocks[:, :, member, :]
        scores = scaling * jnp.einsum(
            "frc,fzc->frz", query_row_set, key_row_set, preferred_element_type=jnp.float32
        )
        scores = jnp.where(allowed, scores, masked_score)
        row_max = jnp.max(scores, axis=-1, keepdims=True)
        exp_scores = jnp.exp(scores - row_max)
        weights = exp_scores / jnp.sum(exp_scores, axis=-1, keepdims=True)
        weights_reduced = weights.astype(jnp.bfloat16)
        attn = jnp.einsum(
            "awv,avq->awq", weights_reduced, value_row_set, preferred_element_type=jnp.float32
        )
        row_dot = jnp.sum(output_grad_rows.astype(jnp.float32) * attn, axis=-1, keepdims=True)
        dweights = jnp.einsum(
            "frc,fzc->frz", output_grad_rows, value_row_set, preferred_element_type=jnp.float32
        )
        score_gradient = (weights * (dweights - row_dot)).astype(jnp.bfloat16)
        dquery = scaling * jnp.einsum(
            "awv,avq->awq", score_gradient, key_row_set, preferred_element_type=jnp.float32
        )
        key_sum = key_sum + scaling * jnp.einsum(
            "ioc,ioa->ica", score_gradient, query_row_set, preferred_element_type=jnp.float32
        )
        value_sum = value_sum + jnp.einsum(
            "ioc,ioa->ica", weights_reduced, output_grad_rows, preferred_element_type=jnp.float32
        )
        attn_list.append(attn)
        dquery_list.append(dquery)
    key_grads = [key_sum]
    value_grads = [value_sum]
    grads = jnp.stack([jnp.stack(key_grads, axis=2), jnp.stack(value_grads, axis=2)])
    grads = grads.reshape(2, block_count, slot_count_all, BLOCK_TOKENS * kv_heads * HEAD_SIZE)
    positions = jnp.arange(2 * block_count)[None, :]
    near_hot = jnp.stack(
        [((near_targets[:, None] == positions) & is_valid[:, 0:1]).astype(jnp.float32)]
    )
    near_sum = jnp.einsum(
        "lqp,sqlx->spx", near_hot, grads[:, :, 1 : 1 + near_count], precision=highest
    )
    own_total = grads[:, :, 0] + near_sum[:, block_count:]
    local_ids = jnp.arange(block_count)[None, :]
    far_parts = []
    for degree in range(far_count):
        column = near_count + degree
        one_hot = (
            (far_targets[degree][:, None] == local_ids) & is_valid[:, column : column + 1]
        ).astype(jnp.float32)
        far_part = jnp.einsum("qp,sqx->spx", one_hot, grads[:, :, 1 + column], precision=highest)
        if degree == 0:
            far_part = far_part + near_sum[:, :block_count]
        far_parts.append(far_part)
    summed = own_total
    for degree in range(far_count):
        summed = summed + from_behind(far_parts[degree], "seq", -(2**degree))
    kv_out = summed.reshape(2, tokens_dev, kv_heads * HEAD_SIZE).astype(jnp.bfloat16)
    attention = (
        jnp.stack(attn_list, axis=2).reshape(tokens_dev, q_heads * HEAD_SIZE).astype(jnp.bfloat16)
    )
    grad_query = (
        jnp.stack(dquery_list, axis=2).reshape(tokens_dev, q_heads * HEAD_SIZE).astype(jnp.bfloat16)
    )
    return (attention, grad_query, kv_out[0], kv_out[1])


def solution(mesh):
    placed = (
        P(("seq", "head"), None),
        P(("seq", "head"), None),
        P(("seq", "head"), None),
        P(("seq", "head"), None),
        P("seq", None),
    )
    return jax.shard_map(
        shards,
        mesh=mesh,
        in_specs=placed,
        out_specs=(P("seq", "head"), P("seq", "head"), P("seq", "head"), P("seq", "head")),
        check_vma=False,
    )
```

profile of v0, /device:TPU:2, one launch (start us, length us, event | category | flops | bytes accessed | tf_op | source)
XLA Modules:
  0.0 144.5 jit_solution(5050257627439415097)
XLA Ops:
  2.1 4.5 %all-to-all-start = ((bf16[32,8,128]{2,0,1:T(8,128)(2,1)}), bf16[32,8,128]{2,0,1:T(8,128)(2,1)S(1)}, u32[]{:S(2)}, u32[]{:S(2)}) async-start(bf16[32,8,128]{2,0,1:T(8,128)(2,1)} %copy_bitcast_fusion.5), calls=%async_computation | async-start | bytes 131072 | tf_op jit(solution)/shard_map/all_to_all | solution.py:22
  7.4 1.7 %fusion.95 = (s32[2]{0:T(128)S(1)}, s32[2]{0:T(128)S(1)}, s32[2]{0:T(128)}, s32[2]{0:T(128)}, s32[2]{0:T(128)}, /*index=5*/s32[2]{0:T(128)}, s32[2]{0:T(128)S(1)...) fusion(s32[2,6]{1,0:T(2,128)} %param.11, s32[]{:T(128)S(6)} %sub.154, ...), kind=kLoop, calls=%fused_computation.221 | loop fusion | flops 32 | bytes 168 | tf_op jit(solution)/shard_map/sub | solution.py:49
  12.9 1.7 %copy.231 = bf16[4,8,8,512]{3,2,0,1:T(8,128)(2,1)} copy(bf16[4,8,8,512]{3,2,1,0:T(8,128)(2,1)} %bitcast.345) | data formatting | bytes 524288 | tf_op jit(solution)/shard_map/all_to_all | solution.py:20
  14.6 2.2 %gather_fusion = pred[896,2]{1,0:T(8,128)(4,1)S(1)} fusion(pred[2,7]{0,1:T(8,128)(4,1)S(1)} %concatenate.9, s32[1024]{0:T(1024)S(1)} %pad_clamp_fusion.6), kind=kCustom, calls=%fused_computation.5 | custom fusion | bytes 7168 | tf_op jit(solution)/shard_map/gather | solution.py:64
  17.0 4.8 %all-to-all-start.1 = ((bf16[32,8,128]{2,0,1:T(8,128)(2,1)}), bf16[32,8,128]{2,0,1:T(8,128)(2,1)S(1)}, u32[]{:S(2)}, u32[]{:S(2)}) async-start(bf16[32,8,128]{2,0,1:T(8,128)(2,1)} %copy_bitcast_fusion.4), calls=%async_computation.1 | async-start | bytes 131072 | tf_op jit(solution)/shard_map/all_to_all | solution.py:23
  21.8 5.6 %all-to-all-done.1 = bf16[32,8,128]{2,0,1:T(8,128)(2,1)S(1)} async-done(((bf16[32,8,128]{2,0,1:T(8,128)(2,1)}), bf16[32,8,128]{2,0,1:T(8,128)(2,1)S(1)}, u32[]{:S(2)}, u32[]{:S(2)}) %all-to-all-start.1) | async-done | bytes 65568 | tf_op jit(solution)/shard_map/all_to_all | solution.py:23
  27.4 3.4 %all-to-all-start.2 = ((bf16[32,8,512]{2,0,1:T(8,128)(2,1)}), bf16[32,8,512]{2,0,1:T(8,128)(2,1)S(1)}, u32[]{:S(2)}, u32[]{:S(2)}) async-start(bf16[32,8,512]{2,0,1:T(8,128)(2,1)} %bitcast.316), calls=%async_computation.2 | async-start | bytes 524288 | tf_op jit(solution)/shard_map/all_to_all | solution.py:20
  30.8 4.0 %collective-permute-start.4 = (bf16[2,256,128]{2,1,0:T(8,128)(2,1)S(1)}, bf16[2,256,128]{2,1,0:T(8,128)(2,1)S(1)}, u32[]{:S(2)}, u32[]{:S(2)}) collective-permute-start(bf16[2,256,128]{2,1,0:T(8,128)(2,1)S(1)} %pad_maximum_fusion.2), channel_id=1, source_target_pairs={{0,128},{8,136},{16,144},{24,152},{32,160},{40,168},{48,176},{56,1... | collective-permute-start | bytes 393224 | tf_op jit(solution)/shard_map/ppermute | solution.py:15
  34.9 1.9 %collective-permute-start.3 = (bf16[2,256,128]{2,1,0:T(8,128)(2,1)S(1)}, bf16[2,256,128]{2,1,0:T(8,128)(2,1)S(1)}, u32[]{:S(2)}, u32[]{:S(2)}) collective-permute-start(bf16[2,256,128]{2,1,0:T(8,128)(2,1)S(1)} %pad_maximum_fusion.2), channel_id=1, source_target_pairs={{0,64},{8,72},{16,80},{24,88},{32,96},{40,104},{48,112},{56,120},{... | collective-permute-start | bytes 393224 | tf_op jit(solution)/shard_map/ppermute | solution.py:15
  36.8 9.1 %collective-permute-start.2 = (bf16[2,256,128]{2,1,0:T(8,128)(2,1)S(1)}, bf16[2,256,128]{2,1,0:T(8,128)(2,1)S(1)}, u32[]{:S(2)}, u32[]{:S(2)}) collective-permute-start(bf16[2,256,128]{2,1,0:T(8,128)(2,1)S(1)} %pad_maximum_fusion.2), channel_id=1, source_target_pairs={{0,32},{8,40},{16,48},{24,56},{32,64},{40,72},{48,80},{56,88},{64,... | collective-permute-start | bytes 393224 | tf_op jit(solution)/shard_map/ppermute | solution.py:15
  45.9 3.4 %collective-permute-start.1 = (bf16[2,256,128]{2,1,0:T(8,128)(2,1)S(1)}, bf16[2,256,128]{2,1,0:T(8,128)(2,1)S(1)}, u32[]{:S(2)}, u32[]{:S(2)}) collective-permute-start(bf16[2,256,128]{2,1,0:T(8,128)(2,1)S(1)} %pad_maximum_fusion.2), channel_id=1, source_target_pairs={{0,16},{8,24},{16,32},{24,40},{32,48},{40,56},{48,64},{56,72},{64,... | collective-permute-start | bytes 393224 | tf_op jit(solution)/shard_map/ppermute | solution.py:15
  49.3 2.9 %collective-permute-start = (bf16[2,256,128]{2,1,0:T(8,128)(2,1)S(1)}, bf16[2,256,128]{2,1,0:T(8,128)(2,1)S(1)}, u32[]{:S(2)}, u32[]{:S(2)}) collective-permute-start(bf16[2,256,128]{2,1,0:T(8,128)(2,1)S(1)} %pad_maximum_fusion.2), channel_id=1, source_target_pairs={{0,8},{8,16},{16,24},{24,32},{32,40},{40,48},{48,56},{56,64},{64,7... | collective-permute-start | bytes 393224 | tf_op jit(solution)/shard_map/ppermute | solution.py:15
  55.0 4.6 %collective-permute-done.1 = bf16[2,256,128]{2,1,0:T(8,128)(2,1)S(1)} collective-permute-done((bf16[2,256,128]{2,1,0:T(8,128)(2,1)S(1)}, bf16[2,256,128]{2,1,0:T(8,128)(2,1)S(1)}, u32[]{:S(2)}, u32[]{:S(2)}) %collective-permute-start.1) | collective-permute-done | bytes 131104 | tf_op jit(solution)/shard_map/ppermute | solution.py:15
  63.2 4.4 %all-to-all-start.3 = ((bf16[32,8,512]{2,0,1:T(8,128)(2,1)}), bf16[32,8,512]{2,0,1:T(8,128)(2,1)S(1)}, u32[]{:S(2)}, u32[]{:S(2)}) async-start(bf16[32,8,512]{2,0,1:T(8,128)(2,1)} %bitcast.315), calls=%async_computation.3 | async-start | bytes 524288 | tf_op jit(solution)/shard_map/all_to_all | solution.py:21
  67.9 7.3 %all-to-all-done.3 = bf16[32,8,512]{2,0,1:T(8,128)(2,1)S(1)} async-done(((bf16[32,8,512]{2,0,1:T(8,128)(2,1)}), bf16[32,8,512]{2,0,1:T(8,128)(2,1)S(1)}, u32[]{:S(2)}, u32[]{:S(2)}) %all-to-all-start.3) | async-done | bytes 262176 | tf_op jit(solution)/shard_map/all_to_all | solution.py:21
  77.2 1.6 %fusion.125 = (f32[2,128]{1,0:T(2,128)S(1)}, f32[2,128,896]{1,2,0:T(8,128)S(1)}) fusion(bf16[2,896,128]{2,1,0:T(8,128)(2,1)S(1)} %bitcast.325, pred[2,896]{1,0:T(4,128)(4,1)S(1)} %copy.119, pred[128,896]{0,1:T(8,128)(4,1)} %fusion.38, bf16[2,128,1,128]{3,2,1,0:T(2,128)(2,1)S(1)} %get-tuple-element.26), kind=kOutput, calls=%fused_computation.251 | convolution fusion | flops 59868032 | bytes 1559296 | tf_op jit(solution)/shard_map/sub | solution.py:81
  78.8 1.6 %fusion.128 = (f32[2,128]{1,0:T(2,128)S(1)}, f32[2,128,896]{1,2,0:T(8,128)S(1)}) fusion(bf16[2,896,128]{2,1,0:T(8,128)(2,1)S(1)} %bitcast.326, pred[2,896]{1,0:T(4,128)(4,1)S(1)} %copy.119, pred[128,896]{0,1:T(8,128)(4,1)} %fusion.38, bf16[2,128,1,128]{3,2,1,0:T(2,128)(2,1)S(1)} %get-tuple-element.23), kind=kOutput, calls=%fused_computation.254 | convolution fusion | flops 59868032 | bytes 1559296 | tf_op jit(solution)/shard_map/sub | solution.py:81
  91.8 2.0 %fusion.127 = (f32[2,128]{1,0:T(2,128)}, f32[2,128,896]{1,2,0:T(8,128)}) fusion(bf16[2,896,128]{2,1,0:T(8,128)(2,1)S(1)} %bitcast.330, pred[2,896]{1,0:T(4,128)(4,1)S(1)} %copy.119, pred[128,896]{0,1:T(8,128)(4,1)S(1)} %copy-done.27, bf16[2,128,1,128]{3,2,1,0:T(2,128)(2,1)S(1)} %copy-done.15), kind=kOutput, calls=%fused_computation.253 | convolution fusion | flops 59868032 | bytes 1559296 | tf_op jit(solution)/shard_map/sub | solution.py:81
  109.0 3.7 %collective-permute-start.6 = (f32[2,2,16384]{2,1,0:T(2,128)S(1)}, f32[2,2,16384]{2,1,0:T(2,128)S(1)}, u32[]{:S(2)}, u32[]{:S(2)}) collective-permute-start(f32[2,2,16384]{2,1,0:T(2,128)S(1)} %convolution_bitcast_fusion.4), channel_id=1, source_target_pairs={{16,0},{24,8},{32,16},{40,24},{48,32},{56,40},{64,48},{72,56},{80,... | collective-permute-start | bytes 786440 | tf_op jit(solution)/shard_map/ppermute | solution.py:15
  113.3 6.5 %collective-permute-start.7 = (f32[2,2,16384]{2,1,0:T(2,128)S(1)}, f32[2,2,16384]{2,1,0:T(2,128)S(1)}, u32[]{:S(2)}, u32[]{:S(2)}) collective-permute-start(f32[2,2,16384]{2,1,0:T(2,128)S(1)} %convolution_bitcast_fusion.3), channel_id=1, source_target_pairs={{32,0},{40,8},{48,16},{56,24},{64,32},{72,40},{80,48},{88,56},{96,... | collective-permute-start | bytes 786440 | tf_op jit(solution)/shard_map/ppermute | solution.py:15
  121.2 1.9 %collective-permute-start.8 = (f32[2,2,16384]{2,1,0:T(2,128)}, f32[2,2,16384]{2,1,0:T(2,128)S(1)}, u32[]{:S(2)}, u32[]{:S(2)}) collective-permute-start(f32[2,2,16384]{2,1,0:T(2,128)} %convolution_bitcast_fusion.2), channel_id=1, source_target_pairs={{64,0},{72,8},{80,16},{88,24},{96,32},{104,40},{112,48},{120,56},{... | collective-permute-start | bytes 786440 | tf_op jit(solution)/shard_map/ppermute | solution.py:15
  127.2 1.9 %collective-permute-start.5 = (f32[2,2,16384]{2,1,0:T(2,128)S(1)}, f32[2,2,16384]{2,1,0:T(2,128)S(1)}, u32[]{:S(2)}, u32[]{:S(2)}) collective-permute-start(f32[2,2,16384]{2,1,0:T(2,128)S(1)} %fusion.4), channel_id=1, source_target_pairs={{8,0},{16,8},{24,16},{32,24},{40,32},{48,40},{56,48},{64,56},{72,6... | collective-permute-start | bytes 786440 | tf_op jit(solution)/shard_map/ppermute | solution.py:15
  131.6 4.5 %collective-permute-done.8 = f32[2,2,16384]{2,1,0:T(2,128)S(1)} collective-permute-done((f32[2,2,16384]{2,1,0:T(2,128)}, f32[2,2,16384]{2,1,0:T(2,128)S(1)}, u32[]{:S(2)}, u32[]{:S(2)}) %collective-permute-start.8) | collective-permute-done | bytes 262176 | tf_op jit(solution)/shard_map/ppermute | solution.py:15
  136.1 5.6 %collective-permute-done.5 = f32[2,2,16384]{2,1,0:T(2,128)S(1)} collective-permute-done((f32[2,2,16384]{2,1,0:T(2,128)S(1)}, f32[2,2,16384]{2,1,0:T(2,128)S(1)}, u32[]{:S(2)}, u32[]{:S(2)}) %collective-permute-start.5) | collective-permute-done | bytes 262176 | tf_op jit(solution)/shard_map/ppermute | solution.py:15
  (193 shorter events, 52.1 us)
Async XLA Ops:
  1.5 51.0 %copy-start.19 = (bf16[32,4096]{1,0:T(8,128)(2,1)S(1)}, bf16[32,4096]{1,0:T(8,128)(2,1)}, u32[]{:S(2)}) copy-start(bf16[32,4096]{1,0:T(8,128)(2,1)} %param.10) | copy-start | bytes 786436
  2.1 14.8 %all-to-all-start = ((bf16[32,8,128]{2,0,1:T(8,128)(2,1)}), bf16[32,8,128]{2,0,1:T(8,128)(2,1)S(1)}, u32[]{:S(2)}, u32[]{:S(2)}) async-start(bf16[32,8,128]{2,0,1:T(8,128)(2,1)} %copy_bitcast_fusion.5), calls=%async_computation | async-start | bytes 131072 | tf_op jit(solution)/shard_map/all_to_all | solution.py:22
  17.0 10.4 %all-to-all-start.1 = ((bf16[32,8,128]{2,0,1:T(8,128)(2,1)}), bf16[32,8,128]{2,0,1:T(8,128)(2,1)S(1)}, u32[]{:S(2)}, u32[]{:S(2)}) async-start(bf16[32,8,128]{2,0,1:T(8,128)(2,1)} %copy_bitcast_fusion.4), calls=%async_computation.1 | async-start | bytes 131072 | tf_op jit(solution)/shard_map/all_to_all | solution.py:23
  27.4 35.8 %all-to-all-start.2 = ((bf16[32,8,512]{2,0,1:T(8,128)(2,1)}), bf16[32,8,512]{2,0,1:T(8,128)(2,1)S(1)}, u32[]{:S(2)}, u32[]{:S(2)}) async-start(bf16[32,8,512]{2,0,1:T(8,128)(2,1)} %bitcast.316), calls=%async_computation.2 | async-start | bytes 524288 | tf_op jit(solution)/shard_map/all_to_all | solution.py:20
  30.8 22.4 %collective-permute-start.4 = (bf16[2,256,128]{2,1,0:T(8,128)(2,1)S(1)}, bf16[2,256,128]{2,1,0:T(8,128)(2,1)S(1)}, u32[]{:S(2)}, u32[]{:S(2)}) collective-permute-start(bf16[2,256,128]{2,1,0:T(8,128)(2,1)S(1)} %pad_maximum_fusion.2), channel_id=1, source_target_pairs={{0,128},{8,136},{16,144},{24,152},{32,160},{40,168},{48,176},{56,1... | collective-permute-start | bytes 393224 | tf_op jit(solution)/shard_map/ppermute | solution.py:15
  34.9 18.9 %collective-permute-start.3 = (bf16[2,256,128]{2,1,0:T(8,128)(2,1)S(1)}, bf16[2,256,128]{2,1,0:T(8,128)(2,1)S(1)}, u32[]{:S(2)}, u32[]{:S(2)}) collective-permute-start(bf16[2,256,128]{2,1,0:T(8,128)(2,1)S(1)} %pad_maximum_fusion.2), channel_id=1, source_target_pairs={{0,64},{8,72},{16,80},{24,88},{32,96},{40,104},{48,112},{56,120},{... | collective-permute-start | bytes 393224 | tf_op jit(solution)/shard_map/ppermute | solution.py:15
  36.8 17.6 %collective-permute-start.2 = (bf16[2,256,128]{2,1,0:T(8,128)(2,1)S(1)}, bf16[2,256,128]{2,1,0:T(8,128)(2,1)S(1)}, u32[]{:S(2)}, u32[]{:S(2)}) collective-permute-start(bf16[2,256,128]{2,1,0:T(8,128)(2,1)S(1)} %pad_maximum_fusion.2), channel_id=1, source_target_pairs={{0,32},{8,40},{16,48},{24,56},{32,64},{40,72},{48,80},{56,88},{64,... | collective-permute-start | bytes 393224 | tf_op jit(solution)/shard_map/ppermute | solution.py:15
  45.9 13.6 %collective-permute-start.1 = (bf16[2,256,128]{2,1,0:T(8,128)(2,1)S(1)}, bf16[2,256,128]{2,1,0:T(8,128)(2,1)S(1)}, u32[]{:S(2)}, u32[]{:S(2)}) collective-permute-start(bf16[2,256,128]{2,1,0:T(8,128)(2,1)S(1)} %pad_maximum_fusion.2), channel_id=1, source_target_pairs={{0,16},{8,24},{16,32},{24,40},{32,48},{40,56},{48,64},{56,72},{64,... | collective-permute-start | bytes 393224 | tf_op jit(solution)/shard_map/ppermute | solution.py:15
  49.3 12.0 %collective-permute-start = (bf16[2,256,128]{2,1,0:T(8,128)(2,1)S(1)}, bf16[2,256,128]{2,1,0:T(8,128)(2,1)S(1)}, u32[]{:S(2)}, u32[]{:S(2)}) collective-permute-start(bf16[2,256,128]{2,1,0:T(8,128)(2,1)S(1)} %pad_maximum_fusion.2), channel_id=1, source_target_pairs={{0,8},{8,16},{16,24},{24,32},{32,40},{40,48},{48,56},{56,64},{64,7... | collective-permute-start | bytes 393224 | tf_op jit(solution)/shard_map/ppermute | solution.py:15
  63.2 12.0 %all-to-all-start.3 = ((bf16[32,8,512]{2,0,1:T(8,128)(2,1)}), bf16[32,8,512]{2,0,1:T(8,128)(2,1)S(1)}, u32[]{:S(2)}, u32[]{:S(2)}) async-start(bf16[32,8,512]{2,0,1:T(8,128)(2,1)} %bitcast.315), calls=%async_computation.3 | async-start | bytes 524288 | tf_op jit(solution)/shard_map/all_to_all | solution.py:21
  76.0 20.1 %copy-start.9 = (bf16[2,128,1,128]{1,3,0,2:T(8,128)(2,1)}, bf16[2,128,1,128]{1,3,0,2:T(8,128)(2,1)S(1)}, u32[]{:S(2)}) copy-start(bf16[2,128,1,128]{1,3,0,2:T(8,128)(2,1)S(1)} %copy.183) | copy-start | bytes 196612
  107.4 12.4 %copy-start.30 = (s32[2]{0:T(128)S(1)}, s32[2]{0:T(128)}, u32[]{:S(2)}) copy-start(s32[2]{0:T(128)} %get-tuple-element.8) | copy-start | bytes 28
  107.5 12.4 %copy-start.34 = (pred[2]{0:T(512)(128)(4,1)S(1)}, pred[2]{0:T(512)(128)(4,1)}, u32[]{:S(2)}) copy-start(pred[2]{0:T(512)(128)(4,1)} %get-tuple-element.39) | copy-start | bytes 10
  107.5 15.7 %copy-start.29 = (s32[2]{0:T(128)S(1)}, s32[2]{0:T(128)}, u32[]{:S(2)}) copy-start(s32[2]{0:T(128)} %get-tuple-element.7) | copy-start | bytes 28
  107.5 15.7 %copy-start.33 = (pred[2]{0:T(512)(128)(4,1)S(1)}, pred[2]{0:T(512)(128)(4,1)}, u32[]{:S(2)}) copy-start(pred[2]{0:T(512)(128)(4,1)} %get-tuple-element.38) | copy-start | bytes 10
  107.5 18.3 %copy-start.28 = (pred[2]{0:T(512)(128)(4,1)S(1)}, pred[2]{0:T(512)(128)(4,1)}, u32[]{:S(2)}) copy-start(pred[2]{0:T(512)(128)(4,1)} %get-tuple-element.42) | copy-start | bytes 10
  108.3 19.0 %copy-start.1 = (f32[2,2,7,16384]{3,1,0,2:T(2,128)}, f32[2,2,7,16384]{3,1,0,2:T(2,128)S(1)}, u32[]{:S(2)}) copy-start(f32[2,2,7,16384]{3,1,0,2:T(2,128)S(1)} %copy_dynamic-update-slice_fusion) | copy-start | bytes 5505028
  108.9 20.2 %copy-start.3 = (bf16[2,128,896]{1,2,0:T(8,128)(2,1)S(1)}, bf16[2,128,896]{1,2,0:T(8,128)(2,1)}, u32[]{:S(2)}) copy-start(bf16[2,128,896]{1,2,0:T(8,128)(2,1)} %copy-done.2) | copy-start | bytes 1376260
  109.0 22.6 %collective-permute-start.6 = (f32[2,2,16384]{2,1,0:T(2,128)S(1)}, f32[2,2,16384]{2,1,0:T(2,128)S(1)}, u32[]{:S(2)}, u32[]{:S(2)}) collective-permute-start(f32[2,2,16384]{2,1,0:T(2,128)S(1)} %convolution_bitcast_fusion.4), channel_id=1, source_target_pairs={{16,0},{24,8},{32,16},{40,24},{48,32},{56,40},{64,48},{72,56},{80,... | collective-permute-start | bytes 786440 | tf_op jit(solution)/shard_map/ppermute | solution.py:15
  113.3 18.3 %collective-permute-start.7 = (f32[2,2,16384]{2,1,0:T(2,128)S(1)}, f32[2,2,16384]{2,1,0:T(2,128)S(1)}, u32[]{:S(2)}, u32[]{:S(2)}) collective-permute-start(f32[2,2,16384]{2,1,0:T(2,128)S(1)} %convolution_bitcast_fusion.3), channel_id=1, source_target_pairs={{32,0},{40,8},{48,16},{56,24},{64,32},{72,40},{80,48},{88,56},{96,... | collective-permute-start | bytes 786440 | tf_op jit(solution)/shard_map/ppermute | solution.py:15
  119.9 9.7 %copy-start.24 = (bf16[2,128,1,128]{3,1,0,2:T(8,128)(2,1)S(1)}, bf16[2,128,1,128]{3,1,0,2:T(8,128)(2,1)}, u32[]{:S(2)}) copy-start(bf16[2,128,1,128]{3,1,0,2:T(8,128)(2,1)} %fusion.34) | copy-start | bytes 196612
  121.2 14.8 %collective-permute-start.8 = (f32[2,2,16384]{2,1,0:T(2,128)}, f32[2,2,16384]{2,1,0:T(2,128)S(1)}, u32[]{:S(2)}, u32[]{:S(2)}) collective-permute-start(f32[2,2,16384]{2,1,0:T(2,128)} %convolution_bitcast_fusion.2), channel_id=1, source_target_pairs={{64,0},{72,8},{80,16},{88,24},{96,32},{104,40},{112,48},{120,56},{... | collective-permute-start | bytes 786440 | tf_op jit(solution)/shard_map/ppermute | solution.py:15
  124.5 11.5 %collective-permute-start.9 = (f32[2,2,16384]{2,1,0:T(2,128)}, f32[2,2,16384]{2,1,0:T(2,128)S(1)}, u32[]{:S(2)}, u32[]{:S(2)}) collective-permute-start(f32[2,2,16384]{2,1,0:T(2,128)} %convolution_bitcast_fusion.1), channel_id=1, source_target_pairs={{128,0},{136,8},{144,16},{152,24},{160,32},{168,40},{176,48},{184,... | collective-permute-start | bytes 786440 | tf_op jit(solution)/shard_map/ppermute | solution.py:15
  127.2 14.4 %collective-permute-start.5 = (f32[2,2,16384]{2,1,0:T(2,128)S(1)}, f32[2,2,16384]{2,1,0:T(2,128)S(1)}, u32[]{:S(2)}, u32[]{:S(2)}) collective-permute-start(f32[2,2,16384]{2,1,0:T(2,128)S(1)} %fusion.4), channel_id=1, source_target_pairs={{8,0},{16,8},{24,16},{32,24},{40,32},{48,40},{56,48},{64,56},{72,6... | collective-permute-start | bytes 786440 | tf_op jit(solution)/shard_map/ppermute | solution.py:15
  (31 other events, 100.5 us)
where the time goes:
time: 146 us; the launch traced here: 145 us
  starting transfers between devices  53.8 us (37%)
  waiting for transfers between devices  28.8 us (20%)
  matrix products  28 us (19%)
  local copies, waits for them, and re-layouts  23.6 us (16%)
  other arithmetic  8.61 us (6%)
  between operations  1.62 us (1%)
    ppermute x10, starting transfers between devices, from_behind(): lax.ppermute(value, axis, [(source, source + steps) for source in range(i...  36.7 us
    ppermute x10, waiting for transfers between devices, from_behind(): lax.ppermute(value, axis, [(source, source + steps) for source in range(i...  15.9 us
    all_to_all x1, waiting for transfers between devices, shards(): lax.all_to_all(output_gradient, 'head', split_axis=1, concat_axis=0, tile...  7.33 us
    sub x4, matrix products, shards(): exp_scores = jnp.exp(scores - row_max)  6.54 us
    all_to_all x1, waiting for transfers between devices, shards(): lax.all_to_all(value_projection, 'head', split_axis=1, concat_axis=0, til...  5.61 us
    unnamed x90, local copies, waits for them, and re-layouts  5.56 us
    all_to_all x1, starting transfers between devices, shards(): lax.all_to_all(value_projection, 'head', split_axis=1, concat_axis=0, til...  4.81 us
    dot_general x5, matrix products, shards(): jnp.einsum('qp,sqx->spx', one_hot, grads[:, :, 1 + column], precision=hig...  4.59 us
  transfers between devices with their start and end apart: 14, of which 6 were waited for; matrix products, arithmetic and copies ran while one was open for 16% of the time, Pallas kernels for 0%

commit v1 on v0

--- a/solution.py
+++ b/solution.py
@@ -7,6 +7,22 @@
 HEAD_SIZE = 128
 BLOCK_TOKENS = 128
 masked_score = -1e30
+
+
+def exchange_in_pairs(value, axis, split, join):
+    ways, here = (lax.axis_size(axis), lax.axis_index(axis))
+    width = value.shape[split] // ways
+    shape = list(value.shape)
+    shape[split] = width
+    height = shape[join]
+    shape[join] = height * ways
+    full = jnp.zeros(shape, value.dtype)
+    for mask in range(ways):
+        part = lax.dynamic_slice_in_dim(value, (here ^ mask) * width, width, axis=split)
+        if mask:
+            part = lax.ppermute(part, axis, [(d, d ^ mask) for d in range(ways)])
+        full = lax.dynamic_update_slice_in_dim(full, part, (here ^ mask) * height, axis=join)
+    return full
 
 
 def from_behind(value, axis, steps):
@@ -19,7 +35,7 @@
     q_local, dout_local, k_local, v_local = (
         lax.all_to_all(query_projection, "head", split_axis=1, concat_axis=0, tiled=True),
         lax.all_to_all(output_gradient, "head", split_axis=1, concat_axis=0, tiled=True),
-        lax.all_to_all(key_projection, "head", split_axis=1, concat_axis=0, tiled=True),
+        exchange_in_pairs(key_projection, "head", 1, 0),
         lax.all_to_all(value_projection, "head", split_axis=1, concat_axis=0, tiled=True),
     )
     tokens_dev = q_local.shape[0]

time: 146 us -> 150 us (1.027)
  starting transfers between devices: 53.8 us -> 60.6 us
  waiting for transfers between devices: 28.8 us -> 26.7 us
    ppermute x0 -> x7, starting transfers between devices: none -> 11.6 us  [exchange_in_pairs(): part = lax.ppermute(part, axis, [(d, d ^ mask) for d in range(ways)])]
    all_to_all x1, waiting for transfers between devices: 5.61 us -> 0.01 us  [shards(): lax.all_to_all(value_projection, 'head', split_axis=1, concat_axis=0, til...]
    all_to_all x1 -> x0, starting transfers between devices: 4.47 us -> none  [shards(): lax.all_to_all(key_projection, 'head', split_axis=1, concat_axis=0, tiled...]
    ppermute x0 -> x7, waiting for transfers between devices: none -> 3.42 us  [exchange_in_pairs(): part = lax.ppermute(part, axis, [(d, d ^ mask) for d in range(ways)])]
  transfers between devices with their start and end apart: 14 -> 20, of which waited for: 6 -> 7; matrix products, arithmetic and copies ran while one was open for 16% -> 15% of each run, Pallas kernels for 0% -> 0%
where the time goes in v1:
time: 150 us; the launch traced here: 149 us
  starting transfers between devices  60.6 us (40%)
  matrix products  28 us (19%)
  waiting for transfers between devices  26.7 us (18%)
  local copies, waits for them, and re-layouts  23 us (15%)
  other arithmetic  8.67 us (6%)
  between operations  1.7 us (1%)
    ppermute x10, starting transfers between devices, from_behind(): lax.ppermute(value, axis, [(source, source + steps) for source in range(i...  36.7 us
    ppermute x10, waiting for transfers between devices, from_behind(): lax.ppermute(value, axis, [(source, source + steps) for source in range(i...  15.9 us
    ppermute x7, starting transfers between devices, exchange_in_pairs(): part = lax.ppermute(part, axis, [(d, d ^ mask) for d in range(ways)])  11.6 us
    all_to_all x1, waiting for transfers between devices, shards(): lax.all_to_all(output_gradient, 'head', split_axis=1, concat_axis=0, tile...  7.33 us
    sub x4, matrix products, shards(): exp_scores = jnp.exp(scores - row_max)  6.57 us
    unnamed x90, local copies, waits for them, and re-layouts  4.73 us
    dot_general x5, matrix products, shards(): jnp.einsum('qp,sqx->spx', one_hot, grads[:, :, 1 + column], precision=hig...  4.62 us
    all_to_all x1, starting transfers between devices, shards(): lax.all_to_all(output_gradient, 'head', split_axis=1, concat_axis=0, tile...  4.46 us
  transfers between devices with their start and end apart: 20, of which 7 were waited for; matrix products, arithmetic and copies ran while one was open for 15% of the time, Pallas kernels for 0%

profile of v1, /device:TPU:2, one launch (start us, length us, event | category | flops | bytes accessed | tf_op | source)
XLA Modules:
  0.0 148.6 jit_solution(2785733351482692148)
XLA Ops:
  1.6 2.5 %collective-permute-start.6 = (bf16[32,128]{1,0:T(8,128)(2,1)S(1)}, bf16[32,128]{1,0:T(8,128)(2,1)S(1)}, u32[]{:S(2)}, u32[]{:S(2)}) collective-permute-start(bf16[32,128]{1,0:T(8,128)(2,1)S(1)} %get-tuple-element.37), channel_id=1, source_target_pairs={{0,7},{1,6},{2,5},{3,4},{4,3},{5,2},{6,1},{7,0},{8,15},{9,14},{10,... | collective-permute-start | bytes 24584 | tf_op jit(solution)/shard_map/ppermute | solution.py:23
  5.0 2.9 %collective-permute-start.3 = (bf16[32,128]{1,0:T(8,128)(2,1)S(1)}, bf16[32,128]{1,0:T(8,128)(2,1)S(1)}, u32[]{:S(2)}, u32[]{:S(2)}) collective-permute-start(bf16[32,128]{1,0:T(8,128)(2,1)S(1)} %get-tuple-element.39), channel_id=1, source_target_pairs={{0,4},{1,5},{2,6},{3,7},{4,0},{5,1},{6,2},{7,3},{8,12},{9,13},{10,... | collective-permute-start | bytes 24584 | tf_op jit(solution)/shard_map/ppermute | solution.py:23
  8.8 3.4 %all-to-all-start = ((bf16[32,8,128]{2,0,1:T(8,128)(2,1)}), bf16[32,8,128]{2,0,1:T(8,128)(2,1)S(1)}, u32[]{:S(2)}, u32[]{:S(2)}) async-start(bf16[32,8,128]{2,0,1:T(8,128)(2,1)} %copy_bitcast_fusion.4), calls=%async_computation | async-start | bytes 131072 | tf_op jit(solution)/shard_map/all_to_all | solution.py:39
  12.9 1.8 %fusion.95 = (s32[2]{0:T(128)S(1)}, s32[2]{0:T(128)S(1)}, s32[2]{0:T(128)}, s32[2]{0:T(128)}, s32[2]{0:T(128)}, /*index=5*/s32[2]{0:T(128)}, s32[2]{0:T(128)S(1)...) fusion(s32[2,6]{1,0:T(2,128)} %param.11, s32[]{:T(128)S(6)} %sub.154, ...), kind=kLoop, calls=%fused_computation.235 | loop fusion | flops 32 | bytes 168 | tf_op jit(solution)/shard_map/sub | solution.py:65
  17.1 2.2 %gather_fusion = pred[896,2]{1,0:T(8,128)(4,1)S(1)} fusion(pred[2,7]{0,1:T(8,128)(4,1)S(1)} %concatenate.9, s32[1024]{0:T(1024)S(1)} %pad_clamp_fusion.6), kind=kCustom, calls=%fused_computation.5 | custom fusion | bytes 7168 | tf_op jit(solution)/shard_map/gather | solution.py:80
  21.8 1.9 %collective-permute-start.1 = (bf16[32,128]{1,0:T(8,128)(2,1)S(1)}, bf16[32,128]{1,0:T(8,128)(2,1)S(1)}, u32[]{:S(2)}, u32[]{:S(2)}) collective-permute-start(bf16[32,128]{1,0:T(8,128)(2,1)S(1)} %get-tuple-element.41), channel_id=1, source_target_pairs={{0,2},{1,3},{2,0},{3,1},{4,6},{5,7},{6,4},{7,5},{8,10},{9,11},{10,... | collective-permute-start | bytes 24584 | tf_op jit(solution)/shard_map/ppermute | solution.py:23
  23.8 1.8 %collective-permute-done.1 = bf16[32,128]{1,0:T(8,128)(2,1)S(1)} collective-permute-done((bf16[32,128]{1,0:T(8,128)(2,1)S(1)}, bf16[32,128]{1,0:T(8,128)(2,1)S(1)}, u32[]{:S(2)}, u32[]{:S(2)}) %collective-permute-start.1) | collective-permute-done | bytes 8224 | tf_op jit(solution)/shard_map/ppermute | solution.py:23
  25.5 3.1 %collective-permute-start.5 = (bf16[32,128]{1,0:T(8,128)(2,1)S(1)}, bf16[32,128]{1,0:T(8,128)(2,1)S(1)}, u32[]{:S(2)}, u32[]{:S(2)}) collective-permute-start(bf16[32,128]{1,0:T(8,128)(2,1)S(1)} %get-tuple-element.43), channel_id=1, source_target_pairs={{0,6},{1,7},{2,4},{3,5},{4,2},{5,3},{6,0},{7,1},{8,14},{9,15},{10,... | collective-permute-start | bytes 24584 | tf_op jit(solution)/shard_map/ppermute | solution.py:23
  30.4 4.4 %all-to-all-start.1 = ((bf16[32,8,512]{2,0,1:T(8,128)(2,1)}), bf16[32,8,512]{2,0,1:T(8,128)(2,1)S(1)}, u32[]{:S(2)}, u32[]{:S(2)}) async-start(bf16[32,8,512]{2,0,1:T(8,128)(2,1)} %bitcast.322), calls=%async_computation.1 | async-start | bytes 524288 | tf_op jit(solution)/shard_map/all_to_all | solution.py:36
  34.9 4.0 %collective-permute-start.11 = (bf16[2,256,128]{2,1,0:T(8,128)(2,1)S(1)}, bf16[2,256,128]{2,1,0:T(8,128)(2,1)S(1)}, u32[]{:S(2)}, u32[]{:S(2)}) collective-permute-start(bf16[2,256,128]{2,1,0:T(8,128)(2,1)S(1)} %pad_maximum_fusion.2), channel_id=1, source_target_pairs={{0,128},{8,136},{16,144},{24,152},{32,160},{40,168},{48,176},{56,1... | collective-permute-start | bytes 393224 | tf_op jit(solution)/shard_map/ppermute | solution.py:31
  38.9 1.9 %collective-permute-start.10 = (bf16[2,256,128]{2,1,0:T(8,128)(2,1)S(1)}, bf16[2,256,128]{2,1,0:T(8,128)(2,1)S(1)}, u32[]{:S(2)}, u32[]{:S(2)}) collective-permute-start(bf16[2,256,128]{2,1,0:T(8,128)(2,1)S(1)} %pad_maximum_fusion.2), channel_id=1, source_target_pairs={{0,64},{8,72},{16,80},{24,88},{32,96},{40,104},{48,112},{56,120},{... | collective-permute-start | bytes 393224 | tf_op jit(solution)/shard_map/ppermute | solution.py:31
  40.8 9.1 %collective-permute-start.9 = (bf16[2,256,128]{2,1,0:T(8,128)(2,1)S(1)}, bf16[2,256,128]{2,1,0:T(8,128)(2,1)S(1)}, u32[]{:S(2)}, u32[]{:S(2)}) collective-permute-start(bf16[2,256,128]{2,1,0:T(8,128)(2,1)S(1)} %pad_maximum_fusion.2), channel_id=1, source_target_pairs={{0,32},{8,40},{16,48},{24,56},{32,64},{40,72},{48,80},{56,88},{64,... | collective-permute-start | bytes 393224 | tf_op jit(solution)/shard_map/ppermute | solution.py:31
  49.9 3.4 %collective-permute-start.8 = (bf16[2,256,128]{2,1,0:T(8,128)(2,1)S(1)}, bf16[2,256,128]{2,1,0:T(8,128)(2,1)S(1)}, u32[]{:S(2)}, u32[]{:S(2)}) collective-permute-start(bf16[2,256,128]{2,1,0:T(8,128)(2,1)S(1)} %pad_maximum_fusion.2), channel_id=1, source_target_pairs={{0,16},{8,24},{16,32},{24,40},{32,48},{40,56},{48,64},{56,72},{64,... | collective-permute-start | bytes 393224 | tf_op jit(solution)/shard_map/ppermute | solution.py:31
  53.3 2.9 %collective-permute-start.7 = (bf16[2,256,128]{2,1,0:T(8,128)(2,1)S(1)}, bf16[2,256,128]{2,1,0:T(8,128)(2,1)S(1)}, u32[]{:S(2)}, u32[]{:S(2)}) collective-permute-start(bf16[2,256,128]{2,1,0:T(8,128)(2,1)S(1)} %pad_maximum_fusion.2), channel_id=1, source_target_pairs={{0,8},{8,16},{16,24},{24,32},{32,40},{40,48},{48,56},{56,64},{64,7... | collective-permute-start | bytes 393224 | tf_op jit(solution)/shard_map/ppermute | solution.py:31
  59.0 4.7 %collective-permute-done.8 = bf16[2,256,128]{2,1,0:T(8,128)(2,1)S(1)} collective-permute-done((bf16[2,256,128]{2,1,0:T(8,128)(2,1)S(1)}, bf16[2,256,128]{2,1,0:T(8,128)(2,1)S(1)}, u32[]{:S(2)}, u32[]{:S(2)}) %collective-permute-start.8) | collective-permute-done | bytes 131104 | tf_op jit(solution)/shard_map/ppermute | solution.py:31
  67.3 4.5 %all-to-all-start.2 = ((bf16[32,8,512]{2,0,1:T(8,128)(2,1)}), bf16[32,8,512]{2,0,1:T(8,128)(2,1)S(1)}, u32[]{:S(2)}, u32[]{:S(2)}) async-start(bf16[32,8,512]{2,0,1:T(8,128)(2,1)} %bitcast.321), calls=%async_computation.2 | async-start | bytes 524288 | tf_op jit(solution)/shard_map/all_to_all | solution.py:37
  72.0 7.3 %all-to-all-done.2 = bf16[32,8,512]{2,0,1:T(8,128)(2,1)S(1)} async-done(((bf16[32,8,512]{2,0,1:T(8,128)(2,1)}), bf16[32,8,512]{2,0,1:T(8,128)(2,1)S(1)}, u32[]{:S(2)}, u32[]{:S(2)}) %all-to-all-start.2) | async-done | bytes 262176 | tf_op jit(solution)/shard_map/all_to_all | solution.py:37
  95.9 2.0 %fusion.127 = (f32[2,128]{1,0:T(2,128)}, f32[2,128,896]{1,2,0:T(8,128)}) fusion(bf16[2,896,128]{2,1,0:T(8,128)(2,1)S(1)} %bitcast.336, pred[2,896]{1,0:T(4,128)(4,1)S(1)} %copy.115, pred[128,896]{0,1:T(8,128)(4,1)S(1)} %copy-done.27, bf16[2,128,1,128]{3,2,1,0:T(2,128)(2,1)S(1)} %copy-done.15), kind=kOutput, calls=%fused_computation.267 | convolution fusion | flops 59868032 | bytes 1559296 | tf_op jit(solution)/shard_map/sub | solution.py:97
  113.0 3.7 %collective-permute-start.13 = (f32[2,2,16384]{2,1,0:T(2,128)S(1)}, f32[2,2,16384]{2,1,0:T(2,128)S(1)}, u32[]{:S(2)}, u32[]{:S(2)}) collective-permute-start(f32[2,2,16384]{2,1,0:T(2,128)S(1)} %convolution_bitcast_fusion.4), channel_id=1, source_target_pairs={{16,0},{24,8},{32,16},{40,24},{48,32},{56,40},{64,48},{72,56},{80,... | collective-permute-start | bytes 786440 | tf_op jit(solution)/shard_map/ppermute | solution.py:31
  117.4 6.5 %collective-permute-start.14 = (f32[2,2,16384]{2,1,0:T(2,128)S(1)}, f32[2,2,16384]{2,1,0:T(2,128)S(1)}, u32[]{:S(2)}, u32[]{:S(2)}) collective-permute-start(f32[2,2,16384]{2,1,0:T(2,128)S(1)} %convolution_bitcast_fusion.3), channel_id=1, source_target_pairs={{32,0},{40,8},{48,16},{56,24},{64,32},{72,40},{80,48},{88,56},{96,... | collective-permute-start | bytes 786440 | tf_op jit(solution)/shard_map/ppermute | solution.py:31
  125.3 1.9 %collective-permute-start.15 = (f32[2,2,16384]{2,1,0:T(2,128)}, f32[2,2,16384]{2,1,0:T(2,128)S(1)}, u32[]{:S(2)}, u32[]{:S(2)}) collective-permute-start(f32[2,2,16384]{2,1,0:T(2,128)} %convolution_bitcast_fusion.2), channel_id=1, source_target_pairs={{64,0},{72,8},{80,16},{88,24},{96,32},{104,40},{112,48},{120,56},{... | collective-permute-start | bytes 786440 | tf_op jit(solution)/shard_map/ppermute | solution.py:31
  131.3 1.9 %collective-permute-start.12 = (f32[2,2,16384]{2,1,0:T(2,128)S(1)}, f32[2,2,16384]{2,1,0:T(2,128)S(1)}, u32[]{:S(2)}, u32[]{:S(2)}) collective-permute-start(f32[2,2,16384]{2,1,0:T(2,128)S(1)} %fusion.4), channel_id=1, source_target_pairs={{8,0},{16,8},{24,16},{32,24},{40,32},{48,40},{56,48},{64,56},{72,6... | collective-permute-start | bytes 786440 | tf_op jit(solution)/shard_map/ppermute | solution.py:31
  135.6 4.5 %collective-permute-done.15 = f32[2,2,16384]{2,1,0:T(2,128)S(1)} collective-permute-done((f32[2,2,16384]{2,1,0:T(2,128)}, f32[2,2,16384]{2,1,0:T(2,128)S(1)}, u32[]{:S(2)}, u32[]{:S(2)}) %collective-permute-start.15) | collective-permute-done | bytes 262176 | tf_op jit(solution)/shard_map/ppermute | solution.py:31
  140.2 5.5 %collective-permute-done.12 = f32[2,2,16384]{2,1,0:T(2,128)S(1)} collective-permute-done((f32[2,2,16384]{2,1,0:T(2,128)S(1)}, f32[2,2,16384]{2,1,0:T(2,128)S(1)}, u32[]{:S(2)}, u32[]{:S(2)}) %collective-permute-start.12) | collective-permute-done | bytes 262176 | tf_op jit(solution)/shard_map/ppermute | solution.py:31
  (214 shorter events, 59.0 us)
Async XLA Ops:
  0.6 55.8 %copy-start.19 = (bf16[32,4096]{1,0:T(8,128)(2,1)S(1)}, bf16[32,4096]{1,0:T(8,128)(2,1)}, u32[]{:S(2)}) copy-start(bf16[32,4096]{1,0:T(8,128)(2,1)} %param.10) | copy-start | bytes 786436
  1.6 28.8 %collective-permute-start.6 = (bf16[32,128]{1,0:T(8,128)(2,1)S(1)}, bf16[32,128]{1,0:T(8,128)(2,1)S(1)}, u32[]{:S(2)}, u32[]{:S(2)}) collective-permute-start(bf16[32,128]{1,0:T(8,128)(2,1)S(1)} %get-tuple-element.37), channel_id=1, source_target_pairs={{0,7},{1,6},{2,5},{3,4},{4,3},{5,2},{6,1},{7,0},{8,15},{9,14},{10,... | collective-permute-start | bytes 24584 | tf_op jit(solution)/shard_map/ppermute | solution.py:23
  4.1 24.7 %collective-permute-start.4 = (bf16[32,128]{1,0:T(8,128)(2,1)S(1)}, bf16[32,128]{1,0:T(8,128)(2,1)S(1)}, u32[]{:S(2)}, u32[]{:S(2)}) collective-permute-start(bf16[32,128]{1,0:T(8,128)(2,1)S(1)} %get-tuple-element.38), channel_id=1, source_target_pairs={{0,5},{1,4},{2,7},{3,6},{4,1},{5,0},{6,3},{7,2},{8,13},{9,12},{10,... | collective-permute-start | bytes 24584 | tf_op jit(solution)/shard_map/ppermute | solution.py:23
  5.0 23.7 %collective-permute-start.3 = (bf16[32,128]{1,0:T(8,128)(2,1)S(1)}, bf16[32,128]{1,0:T(8,128)(2,1)S(1)}, u32[]{:S(2)}, u32[]{:S(2)}) collective-permute-start(bf16[32,128]{1,0:T(8,128)(2,1)S(1)} %get-tuple-element.39), channel_id=1, source_target_pairs={{0,4},{1,5},{2,6},{3,7},{4,0},{5,1},{6,2},{7,3},{8,12},{9,13},{10,... | collective-permute-start | bytes 24584 | tf_op jit(solution)/shard_map/ppermute | solution.py:23
  7.9 20.8 %collective-permute-start.2 = (bf16[32,128]{1,0:T(8,128)(2,1)S(1)}, bf16[32,128]{1,0:T(8,128)(2,1)S(1)}, u32[]{:S(2)}, u32[]{:S(2)}) collective-permute-start(bf16[32,128]{1,0:T(8,128)(2,1)S(1)} %get-tuple-element.40), channel_id=1, source_target_pairs={{0,3},{1,2},{2,1},{3,0},{4,7},{5,6},{6,5},{7,4},{8,11},{9,10},{10,... | collective-permute-start | bytes 24584 | tf_op jit(solution)/shard_map/ppermute | solution.py:23
  7.9 14.0 %collective-permute-start = (bf16[32,128]{1,0:T(8,128)(2,1)S(1)}, bf16[32,128]{1,0:T(8,128)(2,1)S(1)}, u32[]{:S(2)}, u32[]{:S(2)}) collective-permute-start(bf16[32,128]{1,0:T(8,128)(2,1)S(1)} %get-tuple-element.42), channel_id=1, source_target_pairs={{0,1},{1,0},{2,3},{3,2},{4,5},{5,4},{6,7},{7,6},{8,9},{9,8},{10,11... | collective-permute-start | bytes 24584 | tf_op jit(solution)/shard_map/ppermute | solution.py:23
  8.8 21.6 %all-to-all-start = ((bf16[32,8,128]{2,0,1:T(8,128)(2,1)}), bf16[32,8,128]{2,0,1:T(8,128)(2,1)S(1)}, u32[]{:S(2)}, u32[]{:S(2)}) async-start(bf16[32,8,128]{2,0,1:T(8,128)(2,1)} %copy_bitcast_fusion.4), calls=%async_computation | async-start | bytes 131072 | tf_op jit(solution)/shard_map/all_to_all | solution.py:39
  21.8 3.7 %collective-permute-start.1 = (bf16[32,128]{1,0:T(8,128)(2,1)S(1)}, bf16[32,128]{1,0:T(8,128)(2,1)S(1)}, u32[]{:S(2)}, u32[]{:S(2)}) collective-permute-start(bf16[32,128]{1,0:T(8,128)(2,1)S(1)} %get-tuple-element.41), channel_id=1, source_target_pairs={{0,2},{1,3},{2,0},{3,1},{4,6},{5,7},{6,4},{7,5},{8,10},{9,11},{10,... | collective-permute-start | bytes 24584 | tf_op jit(solution)/shard_map/ppermute | solution.py:23
  25.5 4.9 %collective-permute-start.5 = (bf16[32,128]{1,0:T(8,128)(2,1)S(1)}, bf16[32,128]{1,0:T(8,128)(2,1)S(1)}, u32[]{:S(2)}, u32[]{:S(2)}) collective-permute-start(bf16[32,128]{1,0:T(8,128)(2,1)S(1)} %get-tuple-element.43), channel_id=1, source_target_pairs={{0,6},{1,7},{2,4},{3,5},{4,2},{5,3},{6,0},{7,1},{8,14},{9,15},{10,... | collective-permute-start | bytes 24584 | tf_op jit(solution)/shard_map/ppermute | solution.py:23
  30.4 36.9 %all-to-all-start.1 = ((bf16[32,8,512]{2,0,1:T(8,128)(2,1)}), bf16[32,8,512]{2,0,1:T(8,128)(2,1)S(1)}, u32[]{:S(2)}, u32[]{:S(2)}) async-start(bf16[32,8,512]{2,0,1:T(8,128)(2,1)} %bitcast.322), calls=%async_computation.1 | async-start | bytes 524288 | tf_op jit(solution)/shard_map/all_to_all | solution.py:36
  34.9 22.4 %collective-permute-start.11 = (bf16[2,256,128]{2,1,0:T(8,128)(2,1)S(1)}, bf16[2,256,128]{2,1,0:T(8,128)(2,1)S(1)}, u32[]{:S(2)}, u32[]{:S(2)}) collective-permute-start(bf16[2,256,128]{2,1,0:T(8,128)(2,1)S(1)} %pad_maximum_fusion.2), channel_id=1, source_target_pairs={{0,128},{8,136},{16,144},{24,152},{32,160},{40,168},{48,176},{56,1... | collective-permute-start | bytes 393224 | tf_op jit(solution)/shard_map/ppermute | solution.py:31
  38.9 18.9 %collective-permute-start.10 = (bf16[2,256,128]{2,1,0:T(8,128)(2,1)S(1)}, bf16[2,256,128]{2,1,0:T(8,128)(2,1)S(1)}, u32[]{:S(2)}, u32[]{:S(2)}) collective-permute-start(bf16[2,256,128]{2,1,0:T(8,128)(2,1)S(1)} %pad_maximum_fusion.2), channel_id=1, source_target_pairs={{0,64},{8,72},{16,80},{24,88},{32,96},{40,104},{48,112},{56,120},{... | collective-permute-start | bytes 393224 | tf_op jit(solution)/shard_map/ppermute | solution.py:31
  40.8 17.6 %collective-permute-start.9 = (bf16[2,256,128]{2,1,0:T(8,128)(2,1)S(1)}, bf16[2,256,128]{2,1,0:T(8,128)(2,1)S(1)}, u32[]{:S(2)}, u32[]{:S(2)}) collective-permute-start(bf16[2,256,128]{2,1,0:T(8,128)(2,1)S(1)} %pad_maximum_fusion.2), channel_id=1, source_target_pairs={{0,32},{8,40},{16,48},{24,56},{32,64},{40,72},{48,80},{56,88},{64,... | collective-permute-start | bytes 393224 | tf_op jit(solution)/shard_map/ppermute | solution.py:31
  49.9 13.7 %collective-permute-start.8 = (bf16[2,256,128]{2,1,0:T(8,128)(2,1)S(1)}, bf16[2,256,128]{2,1,0:T(8,128)(2,1)S(1)}, u32[]{:S(2)}, u32[]{:S(2)}) collective-permute-start(bf16[2,256,128]{2,1,0:T(8,128)(2,1)S(1)} %pad_maximum_fusion.2), channel_id=1, source_target_pairs={{0,16},{8,24},{16,32},{24,40},{32,48},{40,56},{48,64},{56,72},{64,... | collective-permute-start | bytes 393224 | tf_op jit(solution)/shard_map/ppermute | solution.py:31
  53.3 12.1 %collective-permute-start.7 = (bf16[2,256,128]{2,1,0:T(8,128)(2,1)S(1)}, bf16[2,256,128]{2,1,0:T(8,128)(2,1)S(1)}, u32[]{:S(2)}, u32[]{:S(2)}) collective-permute-start(bf16[2,256,128]{2,1,0:T(8,128)(2,1)S(1)} %pad_maximum_fusion.2), channel_id=1, source_target_pairs={{0,8},{8,16},{16,24},{24,32},{32,40},{40,48},{48,56},{56,64},{64,7... | collective-permute-start | bytes 393224 | tf_op jit(solution)/shard_map/ppermute | solution.py:31
  67.3 12.0 %all-to-all-start.2 = ((bf16[32,8,512]{2,0,1:T(8,128)(2,1)}), bf16[32,8,512]{2,0,1:T(8,128)(2,1)S(1)}, u32[]{:S(2)}, u32[]{:S(2)}) async-start(bf16[32,8,512]{2,0,1:T(8,128)(2,1)} %bitcast.321), calls=%async_computation.2 | async-start | bytes 524288 | tf_op jit(solution)/shard_map/all_to_all | solution.py:37
  80.2 20.0 %copy-start.9 = (bf16[2,128,1,128]{1,3,0,2:T(8,128)(2,1)}, bf16[2,128,1,128]{1,3,0,2:T(8,128)(2,1)S(1)}, u32[]{:S(2)}) copy-start(bf16[2,128,1,128]{1,3,0,2:T(8,128)(2,1)S(1)} %copy.178) | copy-start | bytes 196612
  112.3 19.0 %copy-start.1 = (f32[2,2,7,16384]{3,1,0,2:T(2,128)}, f32[2,2,7,16384]{3,1,0,2:T(2,128)S(1)}, u32[]{:S(2)}) copy-start(f32[2,2,7,16384]{3,1,0,2:T(2,128)S(1)} %copy_dynamic-update-slice_fusion) | copy-start | bytes 5505028
  113.0 20.3 %copy-start.3 = (bf16[2,128,896]{1,2,0:T(8,128)(2,1)S(1)}, bf16[2,128,896]{1,2,0:T(8,128)(2,1)}, u32[]{:S(2)}) copy-start(bf16[2,128,896]{1,2,0:T(8,128)(2,1)} %copy-done.2) | copy-start | bytes 1376260
  113.0 22.6 %collective-permute-start.13 = (f32[2,2,16384]{2,1,0:T(2,128)S(1)}, f32[2,2,16384]{2,1,0:T(2,128)S(1)}, u32[]{:S(2)}, u32[]{:S(2)}) collective-permute-start(f32[2,2,16384]{2,1,0:T(2,128)S(1)} %convolution_bitcast_fusion.4), channel_id=1, source_target_pairs={{16,0},{24,8},{32,16},{40,24},{48,32},{56,40},{64,48},{72,56},{80,... | collective-permute-start | bytes 786440 | tf_op jit(solution)/shard_map/ppermute | solution.py:31
  117.4 18.3 %collective-permute-start.14 = (f32[2,2,16384]{2,1,0:T(2,128)S(1)}, f32[2,2,16384]{2,1,0:T(2,128)S(1)}, u32[]{:S(2)}, u32[]{:S(2)}) collective-permute-start(f32[2,2,16384]{2,1,0:T(2,128)S(1)} %convolution_bitcast_fusion.3), channel_id=1, source_target_pairs={{32,0},{40,8},{48,16},{56,24},{64,32},{72,40},{80,48},{88,56},{96,... | collective-permute-start | bytes 786440 | tf_op jit(solution)/shard_map/ppermute | solution.py:31
  125.3 14.8 %collective-permute-start.15 = (f32[2,2,16384]{2,1,0:T(2,128)}, f32[2,2,16384]{2,1,0:T(2,128)S(1)}, u32[]{:S(2)}, u32[]{:S(2)}) collective-permute-start(f32[2,2,16384]{2,1,0:T(2,128)} %convolution_bitcast_fusion.2), channel_id=1, source_target_pairs={{64,0},{72,8},{80,16},{88,24},{96,32},{104,40},{112,48},{120,56},{... | collective-permute-start | bytes 786440 | tf_op jit(solution)/shard_map/ppermute | solution.py:31
  128.6 11.6 %collective-permute-start.16 = (f32[2,2,16384]{2,1,0:T(2,128)}, f32[2,2,16384]{2,1,0:T(2,128)S(1)}, u32[]{:S(2)}, u32[]{:S(2)}) collective-permute-start(f32[2,2,16384]{2,1,0:T(2,128)} %convolution_bitcast_fusion.1), channel_id=1, source_target_pairs={{128,0},{136,8},{144,16},{152,24},{160,32},{168,40},{176,48},{184,... | collective-permute-start | bytes 786440 | tf_op jit(solution)/shard_map/ppermute | solution.py:31
  131.3 14.4 %collective-permute-start.12 = (f32[2,2,16384]{2,1,0:T(2,128)S(1)}, f32[2,2,16384]{2,1,0:T(2,128)S(1)}, u32[]{:S(2)}, u32[]{:S(2)}) collective-permute-start(f32[2,2,16384]{2,1,0:T(2,128)S(1)} %fusion.4), channel_id=1, source_target_pairs={{8,0},{16,8},{24,16},{32,24},{40,32},{48,40},{56,48},{64,56},{72,6... | collective-permute-start | bytes 786440 | tf_op jit(solution)/shard_map/ppermute | solution.py:31
  (37 other events, 191.2 us)
